TPU v7x, 32 devices: a whole 2x2x4 slice. The times are simulated.
32 devices in a mesh: seq: 16 (over z, y, core), wgt: 2 (over x).
Axes of the slice: x: 2, y: 2, z: 4, core: 2. Of those that a mesh axis runs over, the one named last changes fastest.
Arguments:
- hidden: bfloat16 [6144, 5376], P('seq', 'wgt'), may hold values from -6 to 6
- q_weight: bfloat16 [2, 5376, 2048], P(None, 'seq', 'wgt'), may hold values from -448 to 448, as said below
- k_weight: bfloat16 [2, 5376, 1024], P(None, 'seq', 'wgt'), may hold values from -448 to 448, as said below
- v_weight: bfloat16 [2, 5376, 1024], P(None, 'seq', 'wgt'), may hold values from -448 to 448, as said below
- o_weight: bfloat16 [2, 2048, 5376], P(None, 'seq', 'wgt'), may hold values from -448 to 448, as said below
- q_scale: int32 [2, 42, 16], P(None, None, 'wgt'), may hold values from 113 to 117
- k_scale: int32 [2, 42, 8], P(None, None, 'wgt'), may hold values from 113 to 117
- v_scale: int32 [2, 42, 8], P(None, None, 'wgt'), may hold values from 113 to 117
- o_scale: int32 [2, 16, 42], replicated, may hold values from 113 to 117
- in_gain: float32 [2, 5376], replicated, may hold values from 0.5 to 1.5
- post_gain: float32 [2, 5376], P(None, 'wgt'), may hold values from 0.5 to 1.5
- q_gain: float32 [2, 128], replicated, may hold values from 0.1 to 1.9
- k_gain: float32 [2, 128], replicated, may hold values from 0.1 to 1.9
- windows: int32 [2], replicated, may hold values from 512 to 1024, as said below
Outputs:
- state: bfloat16 [6144, 5376], P('seq', 'wgt')
Inputs may be any that keep to these rules, and one draw needn't show every extreme that they name: `q_weight`: every entry is a finite value of the e4m3 floating-point format: sign, 3 mantissa bits, exponents of that format. `k_weight`: every entry is a finite value of the e4m3 floating-point format. `v_weight`: every entry is a finite value of the e4m3 floating-point format. `o_weight`: every entry is a finite value of the e4m3 floating-point format. `windows`: one layer's window is exactly 1024.
All inputs are finite; a program needn't handle non-finite values.
Results may differ from a plain program's by a relative error of at most 0.0095.
Values may be sent and summed in bfloat16 or wider, within the bound.
No kernel may reach another device: no remote copies, remote signals or barrier semaphores. Data moves between devices by JAX's collectives and lax.ppermute only.
A program may use at most 192 MiB of HBM per device.

v0:
```python
import jax
import jax.numpy as jnp
from jax import lax
from jax.sharding import PartitionSpec as P

HD = 128
BLOCK = 128
WINDOW = 1024
LAYERS = 2


eps = 1e-06
query_scale = 168.0 ** (-0.5)
rope_base = 10000.0


def passed_along(array, axis, by):
    size = lax.axis_size(axis)
    pairs = [(i, i + by) for i in range(size) if 0 <= i + by < size]
    return lax.ppermute(array, axis, pairs)


def rmsnorm(values, gain):
    return values * lax.rsqrt(jnp.mean(values * values, axis=-1, keepdims=True) + eps) * gain


def rotate(values, position):
    half = values.shape[-1] // 2
    inverse = rope_base ** (-jnp.arange(half, dtype=jnp.float32) * 2.0 / values.shape[-1])
    angles = position.astype(jnp.float32)[:, None] * inverse[None, :]
    cosine = jnp.cos(angles)[:, None, :]
    sine = jnp.sin(angles)[:, None, :]
    first = values[..., :half]
    second = values[..., half:]
    return jnp.concatenate(
        [first * cosine - second * sine, second * cosine + first * sine], axis=-1
    )


def expand_scales(scale_codes):
    factor = jnp.exp2(scale_codes.astype(jnp.float32) - 127.0)
    return jnp.repeat(jnp.repeat(factor, BLOCK, axis=0), BLOCK, axis=1).astype(jnp.bfloat16)


def per_device(
    hidden,
    q_weight,
    k_weight,
    v_weight,
    o_weight,
    q_scale,
    k_scale,
    v_scale,
    o_scale,
    in_gain,
    post_gain,
    q_gain,
    k_gain,
    windows,
):
    local_rows = hidden.shape[0]
    width_share = hidden.shape[1]
    model_width = in_gain.shape[1]
    seq_index = lax.axis_index("seq")
    column_offset = lax.axis_index("wgt") * width_share
    halo_count = -(-(WINDOW - 1) // local_rows)
    position = seq_index * local_rows + jnp.arange(local_rows, dtype=jnp.int32)
    key_position = (
        seq_index * local_rows
        - halo_count * local_rows
        + jnp.arange((halo_count + 1) * local_rows, dtype=jnp.int32)
    )
    gap = position[:, None] - key_position[None, :]
    columns = column_offset + jnp.arange(width_share, dtype=jnp.int32)
    pick = (
        (columns // BLOCK)[None, :] == jnp.arange(model_width // BLOCK, dtype=jnp.int32)[:, None]
    ).astype(jnp.float32)
    gathered = (
        lax.all_gather(q_weight, "seq", axis=1, tiled=True),
        lax.all_gather(k_weight, "seq", axis=1, tiled=True),
        lax.all_gather(v_weight, "seq", axis=1, tiled=True),
        lax.all_gather(o_weight, "seq", axis=1, tiled=True),
    )
    state = hidden
    for layer_idx in range(LAYERS):
        outgoing = state
        arriving = lax.all_gather(outgoing, "wgt", axis=1, tiled=True)
        normed = rmsnorm(arriving.astype(jnp.float32), in_gain[layer_idx]).astype(jnp.bfloat16)
        tables = (
            expand_scales(q_scale[layer_idx]),
            expand_scales(k_scale[layer_idx]),
            expand_scales(v_scale[layer_idx]),
        )
        o_factor = jnp.exp2(o_scale[layer_idx].astype(jnp.float32) - 127.0)
        o_columns = jnp.dot(o_factor, pick, precision=lax.Precision.HIGHEST)
        o_table = jnp.repeat(o_columns, BLOCK, axis=0).astype(jnp.bfloat16)
        queries = jnp.dot(
            normed, gathered[0][layer_idx] * tables[0], preferred_element_type=jnp.float32
        )
        key_part = jnp.dot(
            normed, gathered[1][layer_idx] * tables[1], preferred_element_type=jnp.float32
        )
        value_part = jnp.dot(
            normed, gathered[2][layer_idx] * tables[2], preferred_element_type=jnp.float32
        )
        queries = (
            rotate(rmsnorm(queries.reshape(local_rows, -1, HD), q_gain[layer_idx]), position)
            * query_scale
        ).astype(jnp.bfloat16)
        key_heads = rotate(
            rmsnorm(key_part.reshape(local_rows, -1, HD), k_gain[layer_idx]), position
        ).astype(jnp.bfloat16)
        key_flat = key_heads.reshape(local_rows, -1)
        value_flat = value_part.astype(jnp.bfloat16)
        earlier = []
        for distance in range(1, halo_count + 1):
            earlier.insert(0, passed_along((key_flat, value_flat), "seq", distance))
        kv_local = key_flat.shape[1] // HD
        groups = queries.shape[1] // kv_local
        all_keys = jnp.concatenate([item[0] for item in earlier] + [key_flat], axis=0).reshape(
            -1, kv_local, HD
        )
        all_values = jnp.concatenate([item[1] for item in earlier] + [value_flat], axis=0).reshape(
            -1, kv_local, HD
        )
        grouped = queries.reshape(local_rows, kv_local, groups, HD)
        scores = jnp.einsum("qkgd,skd->kgqs", grouped, all_keys, preferred_element_type=jnp.float32)
        allowed = (key_position[None, :] >= 0) & (gap >= 0) & (gap < windows[layer_idx])
        scores = jnp.where(allowed, scores, -1e30)
        top = jnp.max(scores, axis=-1, keepdims=True)
        expval = jnp.exp(scores - top)
        weights = (expval / jnp.sum(expval, axis=-1, keepdims=True)).astype(jnp.bfloat16)
        mixed = jnp.einsum(
            "kgqs,skd->qkgd", weights, all_values, preferred_element_type=jnp.float32
        )
        mixed = mixed.reshape(local_rows, -1).astype(jnp.bfloat16)
        mixed_full = lax.all_gather(mixed, "wgt", axis=1, tiled=True)
        projected = jnp.dot(
            mixed_full, gathered[3][layer_idx] * o_table, preferred_element_type=jnp.float32
        )
        post_squares = lax.psum(jnp.sum(projected * projected, axis=-1), "wgt")
        post = (
            projected
            * lax.rsqrt(post_squares / model_width + eps)[:, None]
            * post_gain[layer_idx][None, :]
        )
        state = (state.astype(jnp.float32) + post).astype(jnp.bfloat16)
    return state


def solution(mesh):
    placed = (
        P("seq", "wgt"),
        P(None, "seq", "wgt"),
        P(None, "seq", "wgt"),
        P(None, "seq", "wgt"),
        P(None, "seq", "wgt"),
        P(None, None, "wgt"),
        P(None, None, "wgt"),
        P(None, None, "wgt"),
        P(),
        P(),
        P(None, "wgt"),
        P(),
        P(),
        P(),
    )
    return jax.shard_map(
        per_device, mesh=mesh, in_specs=placed, out_specs=P("seq", "wgt"), check_vma=False
    )
```

profile of v0, /device:TPU:0, one launch (start us, length us, event | category | flops | bytes accessed | tf_op | source)
XLA Modules:
  0.0 766.7 jit_solution(2744792067710179786)
XLA Ops:
  16.5 51.1 %all-gather.9.cloned.1.call-done = bf16[384,5376]{1,0:T(8,128)(2,1)} async-done(((bf16[384,2688]{1,0:T(8,128)(2,1)}), bf16[384,5376]{1,0:T(8,128)(2,1)}) %all-gather.9.cloned.1.call-update) | async-done | bytes 4128784 | tf_op jit(solution)/shard_map/all_gather | solution.py:87
  70.7 90.0 %all-gather.11.cloned.1.call-done = bf16[2,5376,512]{2,1,0:T(8,128)(2,1)} async-done(((bf16[2,336,512]{2,1,0:T(8,128)(2,1)}), bf16[2,5376,512]{2,1,0:T(8,128)(2,1)}) %all-gather.11.cloned.1.call-update) | async-done | bytes 11010064 | tf_op jit(solution)/shard_map/all_gather | solution.py:81
  161.0 6.8 broadcast_in_dim.41
  167.8 5.5 fusion.49
  181.0 86.7 %all-gather.13.cloned.1.call-done = bf16[2,5376,512]{2,1,0:T(8,128)(2,1)} async-done(((bf16[2,336,512]{2,1,0:T(8,128)(2,1)}), bf16[2,5376,512]{2,1,0:T(8,128)(2,1)}) %all-gather.13.cloned.1.call-update) | async-done | bytes 11010064 | tf_op jit(solution)/shard_map/all_gather | solution.py:80
  267.8 6.8 broadcast_in_dim.44
  274.8 6.8 broadcast_in_dim.101
  286.4 8.2 %copy.42 = bf16[512,5376]{1,0:T(8,128)(2,1)} copy(bf16[512,5376]{0,1:T(8,128)(2,1)} %get-tuple-element.12) | data formatting | bytes 11010048 | tf_op jit(solution)/shard_map/dot_general | solution.py:100
  294.6 6.7 multiply_reduce_fusion.5
  315.5 78.4 %all-gather.15.cloned.1.call-done = bf16[2,5376,1024]{2,1,0:T(8,128)(2,1)} async-done(((bf16[2,336,1024]{2,1,0:T(8,128)(2,1)}), bf16[2,5376,1024]{2,1,0:T(8,128)(2,1)}) %all-gather.15.cloned.1.call-update) | async-done | bytes 22020112 | tf_op jit(solution)/shard_map/all_gather | solution.py:79
  394.1 6.8 broadcast_in_dim.46
  401.0 6.8 broadcast_in_dim.103
  407.8 16.1 %fusion.4 = (bf16[1024,5376]{0,1:T(8,128)(2,1)}, bf16[1024,5376]{0,1:T(8,128)(2,1)}) fusion(bf16[672,8,8,128]{3,2,1,0:T(8,128)(2,1)S(1)} %bitcast.229, bf16[2,5376,1024]{2,1,0:T(8,128)(2,1)} %all-gather.15.cloned.1.call-done, bf16[672,8,8,128]{3,2,1,0:T(8,128)(2,1)S(1)} %bitcast.228), kind=kLoop, calls=%fused_computation.11 | loop fusion | flops 11010048 | bytes 66060288 | tf_op jit(solution)/shard_map/dot_general | solution.py:97
  423.9 14.4 %copy.45 = bf16[1024,5376]{1,0:T(8,128)(2,1)} copy(bf16[1024,5376]{0,1:T(8,128)(2,1)} %get-tuple-element.10) | data formatting | bytes 22020096 | tf_op jit(solution)/shard_map/dot_general | solution.py:97
  438.3 10.3 %multiply_reduce_fusion.3 = (f32[384,8]{0,1:T(8,128)S(1)}, f32[384,8,128]{0,2,1:T(8,128)S(1)}) fusion(bf16[8,128,5376]{2,1,0:T(8,128)(2,1)} %bitcast.235, f32[5376]{0:T(1024)S(1)} %get-tuple-element.6, f32[384]{0:T(512)S(1)} %add_rsqrt_fusion.7, bf16[384,5376]{1,0:T(8,128)(2,1)} %all-gather.9.cloned.1.call-done), kind=kOutput, calls=%fused_computation.85 | convolution fusion | flops 4236899328 | bytes 16747008 | tf_op jit(solution)/shard_map/dot_general | solution.py:97
  452.5 12.5 %fusion.102 = (f32[4,2,384]{2,1,0:T(2,128)S(1)}, f32[4,2,384,1536]{2,3,1,0:T(8,128)}) fusion(pred[384,1536]{0,1:T(8,128)(4,1)S(1)} %get-tuple-element.22, bf16[384,4,128]{0,2,1:T(8,128)(2,1)} %maximum_convert_fusion, bf16[384,4,128]{0,2,1:T(8,128)(2,1)} %bitcast.17, bf16[384,4,128]{0,2,1:T(8,128)(2,1)} %bitcast.16, bf16[384,4,128]{0,2,1:T(8,128)(2,1)} %bitcast.15, ...), kind=kOutput, calls=%fused_computation.180 | convolution fusion | flops 1229587968 | bytes 22622208 | tf_op jit(solution)/shard_map/sub | solution.py:131
  465.0 9.0 %fusion.48 = bf16[4,128,2,384]{3,1,2,0:T(8,128)(2,1)} fusion(bf16[1536,4,128,1]{0,2,3,1:T(8,128)(2,1)S(1)} %bitcast.252, f32[4,2,384,1536]{2,3,1,0:T(8,128)} %get-tuple-element.42, f32[4,2,384]{2,1,0:T(2,128)S(1)} %get-tuple-element.41), kind=kOutput, calls=%fused_computation.87 | convolution fusion | flops 1217789952 | bytes 21245952 | tf_op jit(solution)/shard_map/kgqs,skd->qkgd/dot_general | solution.py:133
  474.6 42.6 %all-gather.19.cloned.1.call-done = bf16[2,2048,2688]{2,1,0:T(8,128)(2,1)} async-done(((bf16[2,128,2688]{2,1,0:T(8,128)(2,1)}), bf16[2,2048,2688]{2,1,0:T(8,128)(2,1)}) %all-gather.19.cloned.1.call-update) | async-done | bytes 22020112 | tf_op jit(solution)/shard_map/all_gather | solution.py:82
  517.2 28.6 %all-gather.17.cloned.1.call-done = bf16[384,2048]{0,1:T(8,128)(2,1)} async-done(((bf16[384,1024]{0,1:T(8,128)(2,1)}), bf16[384,2048]{0,1:T(8,128)(2,1)}) %all-gather.17.cloned.1.call-update) | async-done | bytes 1572880 | tf_op jit(solution)/shard_map/all_gather | solution.py:137
  546.5 11.7 %multiply_reduce_fusion.1 = (f32[384]{0:T(512)S(1)}, f32[384,2688]{1,0:T(8,128)}) fusion(bf16[384,2048]{0,1:T(8,128)(2,1)} %all-gather.17.cloned.1.call-done, bf16[2048,2688]{1,0:T(8,128)(2,1)S(1)} %bitcast.237, bf16[2,2048,2688]{2,1,0:T(8,128)(2,1)} %all-gather.19.cloned.1.call-done), kind=kOutput, calls=%fused_computation.66 | convolution fusion | flops 4235427328 | bytes 27723264 | tf_op jit(solution)/shard_map/dot_general | solution.py:138
  568.3 8.2 %copy.47 = bf16[512,5376]{1,0:T(8,128)(2,1)} copy(bf16[512,5376]{0,1:T(8,128)(2,1)} %get-tuple-element.11) | data formatting | bytes 11010048 | tf_op jit(solution)/shard_map/dot_general | solution.py:100
  576.5 14.1 %copy.50 = bf16[1024,5376]{1,0:T(8,128)(2,1)} copy(bf16[1024,5376]{0,1:T(8,128)(2,1)} %get-tuple-element.9) | data formatting | bytes 22020096 | tf_op jit(solution)/shard_map/dot_general | solution.py:97
  590.6 33.7 %all-gather.21.cloned.1.call-done = bf16[384,5376]{1,0:T(8,128)(2,1)} async-done(((bf16[384,2688]{1,0:T(8,128)(2,1)}), bf16[384,5376]{1,0:T(8,128)(2,1)}) %all-gather.21.cloned.1.call-update) | async-done | bytes 4128784 | tf_op jit(solution)/shard_map/all_gather | solution.py:87
  627.7 5.3 multiply_reduce_fusion.4
  641.9 6.8 broadcast_in_dim.50
  648.7 6.0 fusion.50
  663.3 5.9 multiply_reduce_fusion.2
  678.3 12.3 %fusion.103 = (f32[4,2,384]{2,1,0:T(2,128)S(1)}, f32[4,2,384,1536]{2,3,1,0:T(8,128)}) fusion(pred[384,1536]{0,1:T(8,128)(4,1)} %get-tuple-element.21, bf16[384,4,128]{0,2,1:T(8,128)(2,1)} %maximum_convert_fusion.1, bf16[384,4,128]{0,2,1:T(8,128)(2,1)} %bitcast.50, bf16[384,4,128]{0,2,1:T(8,128)(2,1)} %bitcast.49, bf16[384,4,128]{0,2,1:T(8,128)(2,1)} %bitcast.48, ...), kind=kOutput, calls=%fused_computation.181 | convolution fusion | flops 1229587968 | bytes 22622208 | tf_op jit(solution)/shard_map/sub | solution.py:131
  690.7 8.7 %fusion.47 = bf16[4,128,2,384]{3,1,2,0:T(8,128)(2,1)} fusion(bf16[1536,4,128,1]{0,2,3,1:T(8,128)(2,1)S(1)} %bitcast.253, f32[4,2,384,1536]{2,3,1,0:T(8,128)} %get-tuple-element.50, f32[4,2,384]{2,1,0:T(2,128)S(1)} %get-tuple-element.49), kind=kOutput, calls=%fused_computation.86 | convolution fusion | flops 1217789952 | bytes 21245952 | tf_op jit(solution)/shard_map/kgqs,skd->qkgd/dot_general | solution.py:133
  699.7 31.5 %all-gather.23.cloned.1.call-done = bf16[384,2048]{0,1:T(8,128)(2,1)} async-done(((bf16[384,1024]{0,1:T(8,128)(2,1)}), bf16[384,2048]{0,1:T(8,128)(2,1)}) %all-gather.23.cloned.1.call-update) | async-done | bytes 1572880 | tf_op jit(solution)/shard_map/all_gather | solution.py:137
  736.0 14.3 %multiply_reduce_fusion = (f32[384]{0:T(512)S(1)}, f32[384,2688]{1,0:T(8,128)}) fusion(bf16[384,2048]{0,1:T(8,128)(2,1)S(1)} %copy-done.21, bf16[2048,2688]{1,0:T(8,128)(2,1)} %bitcast.236, bf16[2,2048,2688]{2,1,0:T(8,128)(2,1)} %all-gather.19.cloned.1.call-done), kind=kOutput, calls=%fused_computation.64 | convolution fusion | flops 4235427328 | bytes 27723264 | tf_op jit(solution)/shard_map/dot_general | solution.py:138
  750.3 4.9 psum.15
  (158 shorter events, 94.7 us)
Async XLA Ops:
  6.6 61.1 %all-gather.9.cloned.1.call-start = ((), (), s32[]{:S(2)}) async-start(), calls=%async_computation | async-start | bytes 6193152 | tf_op jit(solution)/shard_map/all_gather | solution.py:87
  7.3 153.5 %all-gather.11.cloned.1.call-start = ((), (), s32[]{:S(2)}) async-start(), calls=%async_computation.1 | async-start | bytes 11698176 | tf_op jit(solution)/shard_map/all_gather | solution.py:81
  8.1 259.6 %all-gather.13.cloned.1.call-start = ((), (), s32[]{:S(2)}) async-start(), calls=%async_computation.2 | async-start | bytes 11698176 | tf_op jit(solution)/shard_map/all_gather | solution.py:80
  8.8 385.1 %all-gather.15.cloned.1.call-start = ((), (), s32[]{:S(2)}) async-start(), calls=%async_computation.3 | async-start | bytes 23396352 | tf_op jit(solution)/shard_map/all_gather | solution.py:79
  9.4 507.8 %all-gather.19.cloned.1.call-start = ((), (), s32[]{:S(2)}) async-start(), calls=%async_computation.5 | async-start | bytes 23396352 | tf_op jit(solution)/shard_map/all_gather | solution.py:82
  10.0 535.8 %all-gather.17.cloned.1.call-start = ((), (), s32[]{:S(2)}) async-start(), calls=%async_computation.4 | async-start | bytes 2359296 | tf_op jit(solution)/shard_map/all_gather | solution.py:137
  173.2 136.3 %collective-permute-start = (bf16[384,512]{1,0:T(8,128)(2,1)S(1)}, bf16[384,512]{1,0:T(8,128)(2,1)S(1)}, u32[]{:S(2)}, u32[]{:S(2)}) collective-permute-start(bf16[384,512]{1,0:T(8,128)(2,1)S(1)} %fusion.49), channel_id=1, source_target_pairs={{0,6},{2,8},{4,10},{6,12},{8,14},{10,16},{12,18},{14,20},{16,22},{... | collective-permute-start | bytes 1179656 | tf_op jit(solution)/shard_map/ppermute | solution.py:20
  175.4 136.6 %collective-permute-start.1 = (bf16[384,512]{1,0:T(8,128)(2,1)S(1)}, bf16[384,512]{1,0:T(8,128)(2,1)S(1)}, u32[]{:S(2)}, u32[]{:S(2)}) collective-permute-start(bf16[384,512]{1,0:T(8,128)(2,1)S(1)} %fusion.49), channel_id=1, source_target_pairs={{0,4},{2,6},{4,8},{6,10},{8,12},{10,14},{12,16},{14,18},{16,20},{1... | collective-permute-start | bytes 1179656 | tf_op jit(solution)/shard_map/ppermute | solution.py:20
  178.9 133.8 %collective-permute-start.2 = (bf16[384,512]{1,0:T(8,128)(2,1)S(1)}, bf16[384,512]{1,0:T(8,128)(2,1)}, u32[]{:S(2)}, u32[]{:S(2)}) collective-permute-start(bf16[384,512]{1,0:T(8,128)(2,1)S(1)} %fusion.49), channel_id=1, source_target_pairs={{0,2},{2,4},{4,6},{6,8},{8,10},{10,12},{12,14},{14,16},{16,18},{18... | collective-permute-start | bytes 1179656 | tf_op jit(solution)/shard_map/ppermute | solution.py:20
  267.8 13.8 %copy-start.1 = (bf16[2,5376,512]{2,1,0:T(8,128)(2,1)S(1)}, bf16[2,5376,512]{2,1,0:T(8,128)(2,1)}, u32[]{:S(2)}) copy-start(bf16[2,5376,512]{2,1,0:T(8,128)(2,1)} %all-gather.13.cloned.1.call-done) | copy-start | bytes 33030148
  302.3 150.1 %collective-permute-start.3 = (bf16[384,512]{0,1:T(8,128)(2,1)}, bf16[384,512]{0,1:T(8,128)(2,1)}, u32[]{:S(2)}, u32[]{:S(2)}) collective-permute-start(bf16[384,512]{0,1:T(8,128)(2,1)} %bitcast.14), channel_id=1, source_target_pairs={{0,6},{2,8},{4,10},{6,12},{8,14},{10,16},{12,18},{14,20},{16,22},{... | collective-permute-start | bytes 1179656 | tf_op jit(solution)/shard_map/ppermute | solution.py:20
  305.3 147.1 %collective-permute-start.4 = (bf16[384,512]{0,1:T(8,128)(2,1)}, bf16[384,512]{0,1:T(8,128)(2,1)}, u32[]{:S(2)}, u32[]{:S(2)}) collective-permute-start(bf16[384,512]{0,1:T(8,128)(2,1)} %bitcast.14), channel_id=1, source_target_pairs={{0,4},{2,6},{4,8},{6,10},{8,12},{10,14},{12,16},{14,18},{16,20},{1... | collective-permute-start | bytes 1179656 | tf_op jit(solution)/shard_map/ppermute | solution.py:20
  309.5 143.0 %collective-permute-start.5 = (bf16[384,512]{0,1:T(8,128)(2,1)}, bf16[384,512]{0,1:T(8,128)(2,1)}, u32[]{:S(2)}, u32[]{:S(2)}) collective-permute-start(bf16[384,512]{0,1:T(8,128)(2,1)} %bitcast.14), channel_id=1, source_target_pairs={{0,2},{2,4},{4,6},{6,8},{8,10},{10,12},{12,14},{14,16},{16,18},{18... | collective-permute-start | bytes 1179656 | tf_op jit(solution)/shard_map/ppermute | solution.py:20
  452.5 12.5 %copy-start.4 = (bf16[1536,512]{0,1:T(8,128)(2,1)S(1)}, bf16[1536,512]{0,1:T(8,128)(2,1)}, u32[]{:S(2)}) copy-start(bf16[1536,512]{0,1:T(8,128)(2,1)} %copy.41) | copy-start | bytes 4718596
  465.0 9.3 %copy-start.10 = (f32[2,2688]{1,0:T(2,128)S(1)}, f32[2,2688]{1,0:T(2,128)}, u32[]{:S(2)}) copy-start(f32[2,2688]{1,0:T(2,128)} %param.24) | copy-start | bytes 64516
  465.0 9.4 %copy-start.22 = (s32[2,16,42]{2,1,0:T(8,128)S(1)}, s32[2,16,42]{2,1,0:T(8,128)}, u32[]{:S(2)}) copy-start(s32[2,16,42]{2,1,0:T(8,128)} %param.22) | copy-start | bytes 16132
  474.0 150.3 %all-gather.21.cloned.1.call-start = ((), (), s32[]{:S(2)}) async-start(), calls=%async_computation.6 | async-start | bytes 6193152 | tf_op jit(solution)/shard_map/all_gather | solution.py:87
  474.2 72.3 %copy-start.11 = (s32[2688]{0:T(1024)}, s32[2688]{0:T(1024)S(1)}, u32[]{:S(2)}) copy-start(s32[2688]{0:T(1024)S(1)} %add_select_fusion) | copy-start | bytes 32260
  568.1 163.2 %all-gather.23.cloned.1.call-start = ((), (), s32[]{:S(2)}) async-start(), calls=%async_computation.7 | async-start | bytes 2359296 | tf_op jit(solution)/shard_map/all_gather | solution.py:137
  634.0 44.3 %collective-permute-start.9 = (bf16[384,512]{0,1:T(8,128)(2,1)}, bf16[384,512]{0,1:T(8,128)(2,1)}, u32[]{:S(2)}, u32[]{:S(2)}) collective-permute-start(bf16[384,512]{0,1:T(8,128)(2,1)} %bitcast.47), channel_id=1, source_target_pairs={{0,6},{2,8},{4,10},{6,12},{8,14},{10,16},{12,18},{14,20},{16,22},{... | collective-permute-start | bytes 1179656 | tf_op jit(solution)/shard_map/ppermute | solution.py:20
  637.4 40.9 %collective-permute-start.10 = (bf16[384,512]{0,1:T(8,128)(2,1)}, bf16[384,512]{0,1:T(8,128)(2,1)}, u32[]{:S(2)}, u32[]{:S(2)}) collective-permute-start(bf16[384,512]{0,1:T(8,128)(2,1)} %bitcast.47), channel_id=1, source_target_pairs={{0,4},{2,6},{4,8},{6,10},{8,12},{10,14},{12,16},{14,18},{16,20},{1... | collective-permute-start | bytes 1179656 | tf_op jit(solution)/shard_map/ppermute | solution.py:20
  641.9 21.4 %slice-start = ((s8[11010048]{0:T(1024)(128)(4,1)}), s8[4194304]{0:T(1024)(128)(4,1)S(1)}, s32[]{:S(2)}) async-start(s8[11010048]{0:T(1024)(128)(4,1)} %bitcast.232), calls=%async_computation.8 | async-start | bytes 8388608
  648.7 14.6 %slice-start.1 = ((s8[11010048]{0:T(1024)(128)(4,1)}), s8[4194304]{0:T(1024)(128)(4,1)S(1)}, s32[]{:S(2)}) async-start(s8[11010048]{0:T(1024)(128)(4,1)} %bitcast.232), calls=%async_computation.9 | async-start | bytes 8388608
  648.7 14.6 %slice-start.2 = ((s8[11010048]{0:T(1024)(128)(4,1)}), s8[2621440]{0:T(1024)(128)(4,1)S(1)}, s32[]{:S(2)}) async-start(s8[11010048]{0:T(1024)(128)(4,1)} %bitcast.232), calls=%async_computation.10 | async-start | bytes 5242880
  654.7 14.9 %collective-permute-start.6 = (bf16[384,512]{1,0:T(8,128)(2,1)}, bf16[384,512]{1,0:T(8,128)(2,1)S(1)}, u32[]{:S(2)}, u32[]{:S(2)}) collective-permute-start(bf16[384,512]{1,0:T(8,128)(2,1)} %fusion.50), channel_id=1, source_target_pairs={{0,6},{2,8},{4,10},{6,12},{8,14},{10,16},{12,18},{14,20},{16,22},{... | collective-permute-start | bytes 1179656 | tf_op jit(solution)/shard_map/ppermute | solution.py:20
  656.9 18.2 %collective-permute-start.7 = (bf16[384,512]{1,0:T(8,128)(2,1)}, bf16[384,512]{1,0:T(8,128)(2,1)}, u32[]{:S(2)}, u32[]{:S(2)}) collective-permute-start(bf16[384,512]{1,0:T(8,128)(2,1)} %fusion.50), channel_id=1, source_target_pairs={{0,4},{2,6},{4,8},{6,10},{8,12},{10,14},{12,16},{14,18},{16,20},{1... | collective-permute-start | bytes 1179656 | tf_op jit(solution)/shard_map/ppermute | solution.py:20
  661.0 14.1 %collective-permute-start.8 = (bf16[384,512]{1,0:T(8,128)(2,1)}, bf16[384,512]{1,0:T(8,128)(2,1)}, u32[]{:S(2)}, u32[]{:S(2)}) collective-permute-start(bf16[384,512]{1,0:T(8,128)(2,1)} %fusion.50), channel_id=1, source_target_pairs={{0,2},{2,4},{4,6},{6,8},{8,10},{10,12},{12,14},{14,16},{16,18},{18... | collective-permute-start | bytes 1179656 | tf_op jit(solution)/shard_map/ppermute | solution.py:20
  669.6 8.7 %collective-permute-start.11 = (bf16[384,512]{0,1:T(8,128)(2,1)}, bf16[384,512]{0,1:T(8,128)(2,1)}, u32[]{:S(2)}, u32[]{:S(2)}) collective-permute-start(bf16[384,512]{0,1:T(8,128)(2,1)} %bitcast.47), channel_id=1, source_target_pairs={{0,2},{2,4},{4,6},{6,8},{8,10},{10,12},{12,14},{14,16},{16,18},{18... | collective-permute-start | bytes 1179656 | tf_op jit(solution)/shard_map/ppermute | solution.py:20
  678.3 12.3 %copy-start.5 = (bf16[1536,512]{0,1:T(8,128)(2,1)S(1)}, bf16[1536,512]{0,1:T(8,128)(2,1)}, u32[]{:S(2)}) copy-start(bf16[1536,512]{0,1:T(8,128)(2,1)} %copy.46) | copy-start | bytes 4718596
  690.6 8.8 %copy-start.12 = (s32[2688]{0:T(1024)S(1)}, s32[2688]{0:T(1024)}, u32[]{:S(2)}) copy-start(s32[2688]{0:T(1024)} %copy-done.11) | copy-start | bytes 32260
  690.6 8.8 %copy-start.23 = (s32[2,16,42]{2,1,0:T(8,128)S(1)}, s32[2,16,42]{2,1,0:T(8,128)}, u32[]{:S(2)}) copy-start(s32[2,16,42]{2,1,0:T(8,128)} %param.22) | copy-start | bytes 16132
  736.0 19.2 %copy-start = (bf16[384,2688]{1,0:T(8,128)(2,1)S(1)}, bf16[384,2688]{1,0:T(8,128)(2,1)}, u32[]{:S(2)}) copy-start(bf16[384,2688]{1,0:T(8,128)(2,1)} %add_convert_fusion.1) | copy-start | bytes 6193156
  (15 other events, 62.9 us)
Sparse Core Ops, SparseCore 0:
  8.9 58.6 all-gather.8
  69.9 90.7 all-gather.10
  163.1 104.5 all-gather.12
  269.0 124.8 all-gather.14
  395.3 121.8 all-gather.18
  518.6 27.1 all-gather.16
  568.2 55.9 all-gather.20
  699.5 31.6 all-gather.22
where the time goes:
time: 775 us; the launch traced here: 767 us
  waiting for transfers between devices  446 us (58%)
  matrix products  109 us (14%)
  local copies, waits for them, and re-layouts  105 us (14%)
  other arithmetic  46 us (6%)
  starting transfers between devices  37.2 us (5%)
  between operations  14.6 us (2%)
  blocking collectives  9.82 us (1%)
    all_gather x1, waiting for transfers between devices, per_device(): lax.all_gather(v_weight, 'seq', axis=1, tiled=True)  90 us
    all_gather x1, waiting for transfers between devices, per_device(): lax.all_gather(k_weight, 'seq', axis=1, tiled=True)  86.7 us
    all_gather x2, waiting for transfers between devices, per_device(): arriving = lax.all_gather(outgoing, 'wgt', axis=1, tiled=True)  84.8 us
    all_gather x1, waiting for transfers between devices, per_device(): lax.all_gather(q_weight, 'seq', axis=1, tiled=True)  78.4 us
    all_gather x2, waiting for transfers between devices, per_device(): mixed_full = lax.all_gather(mixed, 'wgt', axis=1, tiled=True)  60.1 us
    all_gather x1, waiting for transfers between devices, per_device(): lax.all_gather(o_weight, 'seq', axis=1, tiled=True)  42.6 us
    broadcast_in_dim x6, local copies, waits for them, and re-layouts, expand_scales(): jnp.repeat(jnp.repeat(factor, BLOCK, axis=0), BLOCK, axis=1)  40.7 us
    ppermute x12, starting transfers between devices, passed_along(): return lax.ppermute(array, axis, pairs)  36.7 us
  transfers between devices with their start and end apart: 20, of which 8 were waited for; matrix products, arithmetic and copies ran while one was open for 24% of the time, Pallas kernels for 0%

commit v1 on v0

--- a/solution.py
+++ b/solution.py
@@ -1,6 +1,10 @@
+import functools
+
 import jax
 import jax.numpy as jnp
 from jax import lax
+from jax.experimental import pallas as pl
+from jax.experimental.pallas import tpu as pltpu
 from jax.sharding import PartitionSpec as P
 
 HD = 128
@@ -42,7 +46,7 @@
     return jnp.repeat(jnp.repeat(factor, BLOCK, axis=0), BLOCK, axis=1).astype(jnp.bfloat16)
 
 
-def per_device(
+def per_device_plain(
     hidden,
     q_weight,
     k_weight,
@@ -148,6 +152,453 @@
     return state
 
 
+def gated(array, after):
+    if after is None:
+        return array
+    return lax.optimization_barrier((array, after))[0]
+
+
+def ring_pairs(chips):
+    walk = [0] + list(range(1, chips, 2)) + list(range(chips - 2, 0, -2))
+    hops = [(walk[i], walk[(i + 1) % chips]) for i in range(chips)]
+    forward = [(2 * a + core, 2 * b + core) for a, b in hops for core in range(2)]
+    return walk, forward, [(b, a) for a, b in forward]
+
+
+def ring_gather(block, chips, after, holds=()):
+    _, forward, backward = ring_pairs(chips)
+    back = ahead = gated(block, after)
+    steps = []
+    for hop in range(1, chips // 2):
+        back = lax.ppermute(back, "seq", forward)
+        ahead = lax.ppermute(ahead, "seq", backward)
+        steps.append((back, ahead))
+        if hop <= len(holds):
+            back, ahead, _ = lax.optimization_barrier((back, ahead, holds[hop - 1]))
+    half = block.shape[0] // 2
+    far = (lax.ppermute(back[:half], "seq", forward), lax.ppermute(ahead[half:], "seq", backward))
+    return steps, far, steps[min(1, len(steps) - 1)]
+
+
+def swap_pairs(size):
+    return [(i, i ^ 1) for i in range(size)]
+
+
+def project_kernel(at_ref, *refs, counts, heads, scale, in_place, lead):
+    parts, rest = refs[:counts], refs[counts:]
+    states, rest = rest[:4], rest[4:]
+    cos_ref, sin_ref, gain_ref = rest[:3]
+    if lead:
+        out_ref, factor_ref, weight, state, sems = rest[3:]
+    else:
+        factor_ref, out_ref, weight, state, sems = rest[3:]
+    tokens, width = states[0].shape
+    copies = []
+    for i, part in enumerate(parts):
+        begin = pl.multiple_of(at_ref[2 + i], 16)
+        copies.append(pltpu.make_async_copy(part, weight.at[pl.ds(begin, part.shape[0])], sems.at[i]))
+    for i, piece in enumerate(states):
+        copies.append(pltpu.make_async_copy(piece, state.at[i], sems.at[counts + i]))
+    for copy in copies:
+        copy.start()
+    for copy in copies[: counts + 2]:
+        copy.wait()
+    core, wgt = at_ref[0], at_ref[1]
+    own_rows = pl.ds(pl.multiple_of(wgt * width, 128), width)
+    far_rows = pl.ds(pl.multiple_of((1 - wgt) * width, 128), width)
+    for t in range(2):
+        if t == 1:
+            for copy in copies[counts + 2 :]:
+                copy.wait()
+        near, far = state[2 * t], state[2 * t + 1]
+        values = jnp.dot(near, weight[own_rows, :], preferred_element_type=jnp.float32)
+        values = values + jnp.dot(far, weight[far_rows, :], preferred_element_type=jnp.float32)
+        rows = slice(t * tokens, (t + 1) * tokens)
+        if lead:
+            squares = 0.0
+            for piece in (near, far):
+                wide = piece.astype(jnp.float32)
+                squares = squares + jnp.sum(wide * wide, axis=-1, keepdims=True)
+            factor = lax.rsqrt(squares / (2 * width) + eps)
+            factor_ref[rows, :] = jnp.broadcast_to(factor, (tokens, HD))
+        else:
+            factor = factor_ref[rows, :]
+        if in_place:
+            begin = pl.multiple_of(jnp.bitwise_xor(core, t) * tokens, 128)
+        else:
+            begin = t * tokens
+        for h in range(values.shape[1] // HD):
+            columns = slice(h * HD, (h + 1) * HD)
+            value = values[:, columns] * factor
+            if h < heads:
+                value = value * lax.rsqrt(jnp.mean(value * value, axis=-1, keepdims=True) + eps) * gain_ref[...]
+                value = value * cos_ref[rows, :] + pltpu.roll(value, HD // 2, 1) * sin_ref[rows, :]
+                if scale is not None:
+                    value = value * scale
+            out_ref[pl.ds(begin, tokens), columns] = value.astype(jnp.bfloat16)
+
+
+def project(at, parts, states, cosine, sine, gain, factor, heads, scale, in_place):
+    tokens, width = states[0].shape
+    columns = parts[0].shape[1]
+    lead = factor is None
+    anywhere = pl.BlockSpec(memory_space=pl.ANY)
+    local = pl.BlockSpec(memory_space=pltpu.VMEM)
+    out = jax.ShapeDtypeStruct((2 * tokens, columns), jnp.bfloat16)
+    factors = jax.ShapeDtypeStruct((2 * tokens, HD), jnp.float32)
+    return pl.pallas_call(
+        functools.partial(
+            project_kernel, counts=len(parts), heads=heads, scale=scale, in_place=in_place, lead=lead
+        ),
+        in_specs=[pl.BlockSpec(memory_space=pltpu.SMEM)]
+        + [anywhere] * (len(parts) + 4)
+        + [local] * (3 if lead else 4),
+        out_specs=[local, local] if lead else local,
+        out_shape=[out, factors] if lead else out,
+        scratch_shapes=[
+            pltpu.VMEM((2 * width, columns), jnp.bfloat16),
+            pltpu.VMEM((4, tokens, width), jnp.bfloat16),
+            pltpu.SemaphoreType.DMA((len(parts) + 4,)),
+        ],
+        compiler_params=pltpu.CompilerParams(vmem_limit_bytes=32 * 2**20),
+        cost_estimate=pl.CostEstimate(
+            flops=8 * tokens * width * columns,
+            bytes_accessed=8 * tokens * width + 4 * width * columns,
+            transcendentals=tokens,
+        ),
+    )(at, *parts, *states, cosine, sine, gain, *([] if lead else [factor]))
+
+
+def output_kernel(at_ref, *refs, counts):
+    parts, rest = refs[:counts], refs[counts:]
+    pieces, rest = rest[:4], rest[4:]
+    out_ref, squares_ref, weight, mixed, sems = rest
+    tokens, share = pieces[0].shape
+    copies = []
+    for i, piece in enumerate(pieces):
+        copies.append(pltpu.make_async_copy(piece, mixed.at[at_ref[i]], sems.at[counts + i]))
+    for i, part in enumerate(parts):
+        begin = pl.multiple_of(at_ref[4 + i], 16)
+        copies.append(pltpu.make_async_copy(part, weight.at[pl.ds(begin, part.shape[0])], sems.at[i]))
+    for copy in copies:
+        copy.start()
+    for copy in copies:
+        copy.wait()
+    width = out_ref.shape[1]
+    tile = next(t for t in (896, 512, 384, 256, 128) if width % t == 0)
+    squares = jnp.zeros((tokens, 1), jnp.float32)
+    for n in range(width // tile):
+        columns = slice(n * tile, (n + 1) * tile)
+        values = jnp.zeros((tokens, tile), jnp.float32)
+        for p in range(4):
+            values = values + jnp.dot(
+                mixed[p], weight[p * share : (p + 1) * share, columns], preferred_element_type=jnp.float32
+            )
+        out_ref[:, columns] = values
+        squares = squares + jnp.sum(values * values, axis=-1, keepdims=True)
+    squares_ref[...] = jnp.broadcast_to(squares, squares_ref.shape)
+
+
+def output(at, parts, pieces):
+    tokens, share = pieces[0].shape
+    width = parts[0].shape[1]
+    anywhere = pl.BlockSpec(memory_space=pl.ANY)
+    local = pl.BlockSpec(memory_space=pltpu.VMEM)
+    return pl.pallas_call(
+        functools.partial(output_kernel, counts=len(parts)),
+        in_specs=[pl.BlockSpec(memory_space=pltpu.SMEM)] + [anywhere] * (len(parts) + 4),
+        out_specs=[local, local],
+        out_shape=[
+            jax.ShapeDtypeStruct((tokens, width), jnp.float32),
+            jax.ShapeDtypeStruct((tokens, HD), jnp.float32),
+        ],
+        scratch_shapes=[
+            pltpu.VMEM((4 * share, width), jnp.bfloat16),
+            pltpu.VMEM((4, tokens, share), jnp.bfloat16),
+            pltpu.SemaphoreType.DMA((len(parts) + 4,)),
+        ],
+        compiler_params=pltpu.CompilerParams(vmem_limit_bytes=32 * 2**20),
+        cost_estimate=pl.CostEstimate(
+            flops=8 * tokens * width * share, bytes_accessed=12 * share * width, transcendentals=0
+        ),
+    )(at, *parts, *pieces)
+
+
+def attend_kernel(place_ref, q_ref, *refs, reach):
+    kv_refs, out_ref, keys_ref = refs[:-2], refs[-2], refs[-1]
+    tile = q_ref.shape[0]
+    rows = keys_ref.shape[0] - reach
+    kv_heads = keys_ref.shape[1] // (2 * HD)
+    groups = q_ref.shape[1] // (kv_heads * HD)
+    step = pl.program_id(0)
+
+    @pl.when(step == 0)
+    def _():
+        begin = 0
+        for ref in kv_refs:
+            keys_ref[begin : begin + ref.shape[0], :] = ref[...]
+            begin += ref.shape[0]
+
+    core, first, window = place_ref[0], place_ref[1], place_ref[2]
+    steps = rows // (2 * tile)
+    side = (step >= steps).astype(jnp.int32)
+    begin = (jnp.bitwise_xor(core, side) * steps + step - side * steps) * tile
+    begin = pl.multiple_of(begin, tile)
+    span = reach + tile
+    row = lax.broadcasted_iota(jnp.int32, (tile, span), 0)
+    column = lax.broadcasted_iota(jnp.int32, (tile, span), 1)
+    gap = reach + row - column
+    allowed = (gap >= 0) & (gap < window) & (column >= -(first + begin))
+    bias = jnp.where(allowed, 0.0, -1e30).astype(jnp.float32)
+    bias = jnp.concatenate([bias] * groups, axis=0)
+    for g in range(kv_heads):
+        key = keys_ref[pl.ds(begin, span), g * HD : (g + 1) * HD]
+        value = keys_ref[pl.ds(begin, span), (kv_heads + g) * HD : (kv_heads + g + 1) * HD]
+        query = jnp.concatenate(
+            [q_ref[:, (g * groups + j) * HD : (g * groups + j + 1) * HD] for j in range(groups)], axis=0
+        )
+        scores = lax.dot_general(query, key, (((1,), (1,)), ((), ())), preferred_element_type=jnp.float32)
+        scores = scores + bias
+        top = jnp.max(scores, axis=-1, keepdims=True)
+        expval = jnp.exp(scores - top)
+        total = jnp.sum(expval, axis=-1, keepdims=True)
+        mixed = jnp.dot(expval.astype(jnp.bfloat16), value, preferred_element_type=jnp.float32)
+        mixed = (mixed / total).astype(jnp.bfloat16)
+        for j in range(groups):
+            out_ref[:, (g * groups + j) * HD : (g * groups + j + 1) * HD] = mixed[j * tile : (j + 1) * tile]
+
+
+def attend(queries, pieces, place, reach):
+    rows, columns = queries.shape
+    tile = 128
+    width = pieces[0].shape[1]
+    return pl.pallas_call(
+        functools.partial(attend_kernel, reach=reach),
+        grid_spec=pltpu.PrefetchScalarGridSpec(
+            num_scalar_prefetch=1,
+            grid=(rows // tile,),
+            in_specs=[pl.BlockSpec((tile, columns), lambda i, place: (i, 0))]
+            + [pl.BlockSpec(piece.shape, lambda i, place: (0, 0)) for piece in pieces],
+            out_specs=pl.BlockSpec((tile, columns), lambda i, place: (i, 0)),
+            scratch_shapes=[pltpu.VMEM((reach + rows, width), jnp.bfloat16)],
+        ),
+        out_shape=jax.ShapeDtypeStruct((rows, columns), jnp.bfloat16),
+        cost_estimate=pl.CostEstimate(
+            flops=4 * rows * columns * (reach + tile),
+            bytes_accessed=4 * rows * columns,
+            transcendentals=rows * columns // HD * (reach + tile),
+        ),
+    )(place, queries, *pieces)
+
+
+def per_device_pairs(
+    hidden,
+    q_weight,
+    k_weight,
+    v_weight,
+    o_weight,
+    q_scale,
+    k_scale,
+    v_scale,
+    o_scale,
+    in_gain,
+    post_gain,
+    q_gain,
+    k_gain,
+    windows,
+):
+    size = lax.axis_size("seq")
+    chips = size // 2
+    tokens, width = hidden.shape
+    model_width = in_gain.shape[1]
+    place = lax.axis_index("seq")
+    wgt = lax.axis_index("wgt")
+    core = lax.rem(place, 2)
+    chip = place // 2
+    pair = swap_pairs(size)
+    other = [(0, 1), (1, 0)]
+    in_rows = q_weight.shape[1]
+    out_rows = o_weight.shape[1]
+    q_share = q_weight.shape[2] // 2
+    kv_share = k_weight.shape[2] // 2
+    kv_heads = kv_share // HD
+    reach = -(-(WINDOW - 1) // BLOCK) * BLOCK
+
+    walk, _, _ = ring_pairs(chips)
+    spots = jnp.array([walk.index(i) for i in range(chips)], jnp.int32)
+    order = jnp.array(walk, jnp.int32)
+    spot = spots[chip]
+
+    def chip_at(offset):
+        return order[lax.rem(spot + offset + chips, chips)]
+
+    def factors(codes):
+        return jnp.exp2(codes.astype(jnp.float32) - 127.0)
+
+    row_block = (place * in_rows + jnp.arange(in_rows, dtype=jnp.int32)) // BLOCK
+    pick = (row_block[:, None] == jnp.arange(model_width // BLOCK, dtype=jnp.int32)[None, :]).astype(jnp.float32)
+    codes = [scale[layer] for layer in range(LAYERS) for scale in (q_scale, k_scale, v_scale)]
+    in_factors = jnp.dot(pick, factors(jnp.concatenate(codes, axis=1)), precision=lax.Precision.HIGHEST)
+    out_block = (place * out_rows + jnp.arange(out_rows, dtype=jnp.int32)) // BLOCK
+    out_pick = (out_block[:, None] == jnp.arange(o_scale.shape[1], dtype=jnp.int32)[None, :]).astype(jnp.float32)
+    out_codes = lax.dynamic_slice_in_dim(o_scale, wgt * (width // BLOCK), width // BLOCK, 2)
+    out_factors = [
+        jnp.dot(out_pick, factors(out_codes[layer]), precision=lax.Precision.HIGHEST) for layer in range(LAYERS)
+    ]
+
+    def dequantized(weight, factor, gain=None):
+        rows, columns = weight.shape
+        blocks = weight.reshape(rows, columns // BLOCK, BLOCK) * factor.astype(jnp.bfloat16)[:, :, None]
+        if gain is not None:
+            blocks = (blocks.astype(jnp.float32) * gain[:, None, None]).astype(jnp.bfloat16)
+        return blocks.reshape(rows, columns)
+
+    def split(weight):
+        half = weight.shape[1] // 2
+        first, second = weight[:, :half], weight[:, half:]
+        return jnp.where(core == 0, first, second), jnp.where(core == 0, second, first)
+
+    def joined(mine, theirs):
+        return jnp.where(
+            core == 0, jnp.concatenate([mine, theirs], axis=0), jnp.concatenate([theirs, mine], axis=0)
+        )
+
+    own_gains = lax.dynamic_slice_in_dim(in_gain, place * in_rows, in_rows, 1)
+    blocks = []
+    begin = 0
+    for layer in range(LAYERS):
+        parts = []
+        for weight in (q_weight, k_weight, v_weight):
+            count = weight.shape[2] // BLOCK
+            factor = in_factors[:, begin : begin + count]
+            parts.append(split(dequantized(weight[layer], factor, own_gains[layer])))
+            begin += count
+        (q_mine, q_theirs), (k_mine, k_theirs), (v_mine, v_theirs) = parts
+        kv_theirs = lax.ppermute(jnp.concatenate([k_theirs, v_theirs], axis=1), "seq", pair)
+        kv_block = joined(jnp.concatenate([k_mine, v_mine], axis=1), kv_theirs)
+        q_block = joined(q_mine, lax.ppermute(q_theirs, "seq", pair))
+        blocks += [kv_block, q_block, dequantized(o_weight[layer], out_factors[layer])]
+    gathered = []
+    after = None
+    for number, block in enumerate(blocks):
+        holds = (tuple(blocks[1:2]), tuple(blocks[2:])) if number == 0 else ()
+        steps, far, after = ring_gather(block, chips, after, holds)
+        gathered.append((block, steps, far))
+
+    def own_first(own, pal):
+        return jnp.concatenate([own, pal], axis=0)
+
+    local = jnp.arange(tokens, dtype=jnp.int32)
+    position = own_first(place * tokens + local, (place + 1 - 2 * core) * tokens + local)
+    half = HD // 2
+    inverse = rope_base ** (-jnp.arange(half, dtype=jnp.float32) * 2.0 / HD)
+    angles = position.astype(jnp.float32)[:, None] * inverse[None, :]
+    cosine, sine = jnp.cos(angles), jnp.sin(angles)
+    cosine = jnp.concatenate([cosine, cosine], axis=1)
+    sine = jnp.concatenate([-sine, sine], axis=1)
+    first_key = chip * (2 * tokens) - reach
+
+    def laid(gathered_block, rows):
+        block, steps, far = gathered_block
+        parts, begins = [block], [chip_at(0) * rows]
+        for i, (back, ahead) in enumerate(steps):
+            parts += [back, ahead]
+            begins += [chip_at(-(i + 1)) * rows, chip_at(i + 1) * rows]
+        farthest = chip_at(chips // 2) * rows
+        parts += list(far)
+        begins += [farthest, farthest + far[0].shape[0]]
+        return parts, begins
+
+    def scalars(values):
+        return jnp.stack([jnp.asarray(value, jnp.int32) for value in values])
+
+    state = hidden
+    for layer in range(LAYERS):
+        kv_gathered, q_gathered, o_gathered = gathered[3 * layer : 3 * layer + 3]
+        far_state = lax.ppermute(state, "wgt", other)
+        pal_state = lax.ppermute(state, "seq", pair)
+        pal_far_state = lax.ppermute(far_state, "seq", pair)
+        states = [state, far_state, pal_state, pal_far_state]
+        parts, begins = laid(kv_gathered, 2 * in_rows)
+        kv, factor = project(
+            scalars([core, wgt] + begins),
+            parts,
+            states,
+            cosine,
+            sine,
+            k_gain[layer][None, :],
+            None,
+            kv_heads,
+            None,
+            True,
+        )
+        pieces = [kv]
+        rest = reach
+        distance = 1
+        while rest > 0:
+            rows = min(rest, 2 * tokens)
+            pairs = [(i, i + 2 * distance) for i in range(size - 2 * distance)]
+            pieces.insert(0, lax.ppermute(kv[2 * tokens - rows :], "seq", pairs))
+            rest -= rows
+            distance += 1
+        parts, begins = laid(q_gathered, 2 * in_rows)
+        queries = project(
+            scalars([core, wgt] + begins),
+            parts,
+            states,
+            cosine,
+            sine,
+            q_gain[layer][None, :],
+            factor,
+            q_share // HD,
+            query_scale,
+            False,
+        )
+        mixed = attend(queries, pieces, scalars([core, first_key, windows[layer]]), reach)
+        near = mixed[:tokens]
+        near_pal = lax.ppermute(mixed[tokens:], "seq", pair)
+        far_mixed = lax.ppermute(near, "wgt", other)
+        far_pal = lax.ppermute(near_pal, "wgt", other)
+        spots_of = [
+            jnp.bitwise_xor(wgt, i // 2) * 2 + jnp.bitwise_xor(core, i % 2) for i in range(4)
+        ]
+        parts, begins = laid(o_gathered, 2 * out_rows)
+        theirs = [lax.ppermute(part, "seq", pair) for part in parts]
+        own_begins = [begin + core * out_rows for begin in begins]
+        their_begins = [begin + (1 - core) * out_rows for begin in begins]
+        projected, squares = output(
+            scalars(spots_of + own_begins + their_begins), parts + theirs, [near, near_pal, far_mixed, far_pal]
+        )
+        squares = squares[:, 0].reshape(-1, HD)
+        squares = (squares + lax.ppermute(squares, "wgt", other)).reshape(-1)
+        post = projected * lax.rsqrt(squares / model_width + eps)[:, None] * post_gain[layer][None, :]
+        state = (state.astype(jnp.float32) + post).astype(jnp.bfloat16)
+    return state
+
+
+def fits_pairs(size, wgts, shapes):
+    tokens, width = shapes[0]
+    return (
+        wgts == 2
+        and size % 4 == 0
+        and tokens % 128 == 0
+        and width % BLOCK == 0
+        and shapes[1][2] % (2 * HD) == 0
+        and shapes[2][2] % (2 * HD) == 0
+        and (shapes[1][2] // 2) % shapes[4][1] == 0
+        and shapes[4][1] % 32 == 0
+        and shapes[1][1] % 16 == 0
+        and (2 * width) % size == 0
+    )
+
+
+def per_device(*arrays):
+    shapes = [array.shape for array in arrays]
+    if fits_pairs(lax.axis_size("seq"), lax.axis_size("wgt"), shapes):
+        return per_device_pairs(*arrays)
+    return per_device_plain(*arrays)
+
+
 def solution(mesh):
     placed = (
         P("seq", "wgt"),

time: 775 us -> 506 us (0.65)
  the two profiles are of different devices: /device:TPU:0 before, /device:TPU:20 now
where the time goes in v1:
time: 506 us; the launch traced here: 497 us
  waiting for transfers between devices  254 us (50%)
  Pallas kernels  84.9 us (17%)
  starting transfers between devices  73.1 us (14%)
  local copies, waits for them, and re-layouts  42.3 us (8%)
  other arithmetic  25.7 us (5%)
  between operations  16.3 us (3%)
    ppermute x18, waiting for transfers between devices, ring_gather(): back = lax.ppermute(back, 'seq', forward)  124 us
    ppermute x6, waiting for transfers between devices, ring_gather(): lax.ppermute(back[:half], 'seq', forward)  56.6 us
    pallas_call x4, Pallas kernels, project(): pl.pallas_call(functools.partial(project_kernel, counts=len(parts), heads...  41.3 us
    pallas_call x2, Pallas kernels, attend(): pl.pallas_call(functools.partial(attend_kernel, reach=reach), grid_spec=p...  23.7 us
    ppermute x18, starting transfers between devices, ring_gather(): ahead = lax.ppermute(ahead, 'seq', backward)  21.6 us
    ppermute x18, waiting for transfers between devices, ring_gather(): ahead = lax.ppermute(ahead, 'seq', backward)  21.1 us
    pallas_call x2, Pallas kernels, output(): pl.pallas_call(functools.partial(output_kernel, counts=len(parts)), in_sp...  19.9 us
    unnamed x114, local copies, waits for them, and re-layouts  18.1 us
  transfers between devices with their start and end apart: 88, of which 36 were waited for; matrix products, arithmetic and copies ran while one was open for 10% of the time, Pallas kernels for 13%

profile of v1, /device:TPU:20, one launch (start us, length us, event | category | flops | bytes accessed | tf_op | source)
XLA Modules:
  0.0 497.0 jit_solution(13920704192596291018)
XLA Ops:
  23.1 11.2 %collective-permute-done.2.refs_1_ = bf16[672,512]{1,0:T(8,128)(2,1)} collective-permute-done((bf16[672,512]{1,0:T(8,128)(2,1)S(1)}, bf16[672,512]{1,0:T(8,128)(2,1)}, u32[]{:S(2)}, u32[]{:S(2)}) %collective-permute-start.2) | collective-permute-done | bytes 688160 | tf_op jit(solution)/shard_map/ppermute | solution.py:173
  45.9 6.6 %collective-permute-done.4.refs_3_ = bf16[672,512]{1,0:T(8,128)(2,1)S(1)} collective-permute-done((bf16[672,512]{1,0:T(8,128)(2,1)}, bf16[672,512]{1,0:T(8,128)(2,1)S(1)}, u32[]{:S(2)}, u32[]{:S(2)}) %collective-permute-start.4) | collective-permute-done | bytes 688160 | tf_op jit(solution)/shard_map/ppermute | solution.py:173
  60.7 10.6 %collective-permute-done.6.refs_1_ = bf16[672,512]{1,0:T(8,128)(2,1)} collective-permute-done((bf16[672,512]{1,0:T(8,128)(2,1)S(1)}, bf16[672,512]{1,0:T(8,128)(2,1)}, u32[]{:S(2)}, u32[]{:S(2)}) %collective-permute-start.6) | collective-permute-done | bytes 688160 | tf_op jit(solution)/shard_map/ppermute | solution.py:173
  75.0 11.1 %collective-permute-done.36.refs_5_ = bf16[672,512]{1,0:T(8,128)(2,1)} collective-permute-done((bf16[672,512]{1,0:T(8,128)(2,1)S(1)}, bf16[672,512]{1,0:T(8,128)(2,1)}, u32[]{:S(2)}, u32[]{:S(2)}) %collective-permute-start.36) | collective-permute-done | bytes 688160 | tf_op jit(solution)/shard_map/ppermute | solution.py:173
  109.0 16.9 %collective-permute-done.38.refs_7_ = bf16[336,512]{1,0:T(8,128)(2,1)S(1)} collective-permute-done((bf16[336,512]{1,0:T(8,128)(2,1)S(1)}, bf16[336,512]{1,0:T(8,128)(2,1)S(1)}, u32[]{:S(2)}, u32[]{:S(2)}) %collective-permute-start.38) | collective-permute-done | bytes 344096 | tf_op jit(solution)/shard_map/ppermute | solution.py:179
  128.7 8.2 %collective-permute-done.39.refs_8_ = bf16[336,512]{1,0:T(8,128)(2,1)S(1)} collective-permute-done((bf16[336,512]{1,0:T(8,128)(2,1)S(1)}, bf16[336,512]{1,0:T(8,128)(2,1)S(1)}, u32[]{:S(2)}, u32[]{:S(2)}) %collective-permute-start.39) | collective-permute-done | bytes 344096 | tf_op jit(solution)/shard_map/ppermute | solution.py:179
  142.7 10.4 %shard_map.154 = (bf16[768,512]{1,0:T(8,128)(2,1)}, f32[768,128]{1,0:T(8,128)S(1)}) custom-call(s32[11]{0:T(128)S(1)} %stack.85.at_ref, bf16[672,512]{1,0:T(8,128)(2,1)S(1)} %copy-done.15, bf16[672,512]{1,0:T(8,128)(2,1)} %collective-permute-done.2.refs_1_, bf16[672,512]{1,0:T(8,128)(2,1)} %collective-permute-done.3.refs_2_, ...), custom_call_target="tpu_custom_call" | custom-call | flops 4227858432 | bytes 13762560 | tf_op jit(solution)/shard_map/pallas_call | solution.py:249
  170.2 9.9 %shard_map.155.q_ref = bf16[768,512]{1,0:T(8,128)(2,1)S(1)} custom-call(s32[11]{0:T(128)S(1)} %stack.85.at_ref, bf16[672,512]{1,0:T(8,128)(2,1)S(1)} %copy-done.3, bf16[672,512]{1,0:T(8,128)(2,1)} %collective-permute-done.6.refs_1_, bf16[672,512]{1,0:T(8,128)(2,1)} %collective-permute-done.8.refs_2_, bf16[672,512]{1,0:T(8,128)(2,1)} %collective-permute-done.7.refs_3_, ...), custom_call_target="tpu_custom_call" | custom-call | flops 4227858432 | bytes 13762560 | tf_op jit(solution)/shard_map/pallas_call | solution.py:249
  181.0 4.3 collective-permute-done.40.refs_0_
  187.3 11.8 %shard_map.156 = bf16[768,512]{1,0:T(8,128)(2,1)} custom-call(s32[3]{0:T(128)} %pad_add_fusion.place_ref, bf16[768,512]{1,0:T(8,128)(2,1)} %copy-done.11, bf16[256,512]{1,0:T(8,128)(2,1)} %copy-done.54, bf16[768,512]{1,0:T(8,128)(2,1)} %collective-permute-done.41.refs_1_, bf16[768,512]{1,0:T(8,128)(2,1)} %get-tuple-element.29.refs_2_), custom_call_target="tpu_custom_call" | custom-call | flops 1811939328 | bytes 1572864 | tf_op jit(solution)/shard_map/pallas_call | solution.py:375
  200.9 7.1 %collective-permute-done.15.refs_6_ = bf16[128,2688]{1,0:T(8,128)(2,1)S(1)} collective-permute-done((bf16[128,2688]{1,0:T(8,128)(2,1)}, bf16[128,2688]{1,0:T(8,128)(2,1)S(1)}, u32[]{:S(2)}, u32[]{:S(2)}) %collective-permute-start.15) | collective-permute-done | bytes 688160 | tf_op jit(solution)/shard_map/ppermute | solution.py:174
  212.3 6.6 %collective-permute-done.43.refs_20_ = bf16[384,512]{1,0:T(8,128)(2,1)S(1)} collective-permute-done((bf16[384,512]{1,0:T(8,128)(2,1)S(1)}, bf16[384,512]{1,0:T(8,128)(2,1)S(1)}, u32[]{:S(2)}, u32[]{:S(2)}) %collective-permute-start.43) | collective-permute-done | bytes 393248 | tf_op jit(solution)/shard_map/ppermute | solution.py:560
  225.8 4.4 collective-permute-done.44.refs_21_
  232.3 10.1 %shard_map.157 = (f32[384,2688]{1,0:T(8,128)S(1)}, f32[384,128]{1,0:T(8,128)S(1)}) custom-call(s32[22]{0:T(128)S(1)} %stack.80.at_ref, bf16[128,2688]{1,0:T(8,128)(2,1)} %get-tuple-element.25.refs_0_, bf16[128,2688]{1,0:T(8,128)(2,1)} %collective-permute-done.10.refs_1_, bf16[128,2688]{1,0:T(8,128)(2,1)} %collective-permute-done.11.refs_2_, ...), custom_call_target="tpu_custom_call" | custom-call | flops 4227858432 | bytes 16515072 | tf_op jit(solution)/shard_map/pallas_call | solution.py:307
  248.2 11.2 %collective-permute-done.46.refs_1_ = bf16[672,512]{1,0:T(8,128)(2,1)S(1)} collective-permute-done((bf16[672,512]{1,0:T(8,128)(2,1)S(1)}, bf16[672,512]{1,0:T(8,128)(2,1)S(1)}, u32[]{:S(2)}, u32[]{:S(2)}) %collective-permute-start.46) | collective-permute-done | bytes 688160 | tf_op jit(solution)/shard_map/ppermute | solution.py:173
  261.4 12.5 %collective-permute-done.47.refs_3_ = bf16[672,512]{1,0:T(8,128)(2,1)S(1)} collective-permute-done((bf16[672,512]{1,0:T(8,128)(2,1)S(1)}, bf16[672,512]{1,0:T(8,128)(2,1)S(1)}, u32[]{:S(2)}, u32[]{:S(2)}) %collective-permute-start.47) | collective-permute-done | bytes 688160 | tf_op jit(solution)/shard_map/ppermute | solution.py:173
  277.9 11.6 %collective-permute-done.50.refs_1_ = bf16[672,512]{1,0:T(8,128)(2,1)S(1)} collective-permute-done((bf16[672,512]{1,0:T(8,128)(2,1)S(1)}, bf16[672,512]{1,0:T(8,128)(2,1)S(1)}, u32[]{:S(2)}, u32[]{:S(2)}) %collective-permute-start.50) | collective-permute-done | bytes 688160 | tf_op jit(solution)/shard_map/ppermute | solution.py:173
  291.8 13.2 %collective-permute-done.51.refs_3_ = bf16[672,512]{1,0:T(8,128)(2,1)S(1)} collective-permute-done((bf16[672,512]{1,0:T(8,128)(2,1)S(1)}, bf16[672,512]{1,0:T(8,128)(2,1)S(1)}, u32[]{:S(2)}, u32[]{:S(2)}) %collective-permute-start.51) | collective-permute-done | bytes 688160 | tf_op jit(solution)/shard_map/ppermute | solution.py:173
  307.9 15.5 %collective-permute-done.54.refs_1_ = bf16[128,2688]{1,0:T(8,128)(2,1)} collective-permute-done((bf16[128,2688]{1,0:T(8,128)(2,1)S(1)}, bf16[128,2688]{1,0:T(8,128)(2,1)}, u32[]{:S(2)}, u32[]{:S(2)}) %collective-permute-start.54) | collective-permute-done | bytes 688160 | tf_op jit(solution)/shard_map/ppermute | solution.py:173
  324.3 13.8 %collective-permute-done.78.refs_5_ = bf16[672,512]{1,0:T(8,128)(2,1)S(1)} collective-permute-done((bf16[672,512]{1,0:T(8,128)(2,1)S(1)}, bf16[672,512]{1,0:T(8,128)(2,1)S(1)}, u32[]{:S(2)}, u32[]{:S(2)}) %collective-permute-start.78) | collective-permute-done | bytes 688160 | tf_op jit(solution)/shard_map/ppermute | solution.py:173
  340.3 17.1 %collective-permute-done.80.refs_7_ = bf16[336,512]{1,0:T(8,128)(2,1)S(1)} collective-permute-done((bf16[336,512]{1,0:T(8,128)(2,1)S(1)}, bf16[336,512]{1,0:T(8,128)(2,1)S(1)}, u32[]{:S(2)}, u32[]{:S(2)}) %collective-permute-start.80) | collective-permute-done | bytes 344096 | tf_op jit(solution)/shard_map/ppermute | solution.py:179
  361.5 10.3 %shard_map.158 = (bf16[768,512]{1,0:T(8,128)(2,1)S(1)}, f32[768,128]{1,0:T(8,128)S(1)}) custom-call(s32[11]{0:T(128)S(1)} %stack.85.at_ref, bf16[672,512]{1,0:T(8,128)(2,1)S(1)} %copy-done.13, bf16[672,512]{1,0:T(8,128)(2,1)S(1)} %collective-permute-done.46.refs_1_, bf16[672,512]{1,0:T(8,128)(2,1)S(1)} %collective-permute-done.48.refs_2_, ...), custom_call_target="tpu_custom_call" | custom-call | flops 4227858432 | bytes 13762560 | tf_op jit(solution)/shard_map/pallas_call | solution.py:249
  380.9 6.9 %collective-permute-done.72.refs_6_ = bf16[672,512]{1,0:T(8,128)(2,1)S(1)} collective-permute-done((bf16[672,512]{1,0:T(8,128)(2,1)S(1)}, bf16[672,512]{1,0:T(8,128)(2,1)S(1)}, u32[]{:S(2)}, u32[]{:S(2)}) %collective-permute-start.72) | collective-permute-done | bytes 688160 | tf_op jit(solution)/shard_map/ppermute | solution.py:174
  392.5 17.4 %collective-permute-done.73.refs_7_ = bf16[336,512]{1,0:T(8,128)(2,1)S(1)} collective-permute-done((bf16[336,512]{1,0:T(8,128)(2,1)S(1)}, bf16[336,512]{1,0:T(8,128)(2,1)S(1)}, u32[]{:S(2)}, u32[]{:S(2)}) %collective-permute-start.73) | collective-permute-done | bytes 344096 | tf_op jit(solution)/shard_map/ppermute | solution.py:179
  420.9 10.8 %shard_map.159.q_ref = bf16[768,512]{1,0:T(8,128)(2,1)S(1)} custom-call(s32[11]{0:T(128)S(1)} %stack.85.at_ref, bf16[672,512]{1,0:T(8,128)(2,1)S(1)} %maximum_select_fusion.3.refs_0_, bf16[672,512]{1,0:T(8,128)(2,1)S(1)} %collective-permute-done.50.refs_1_, bf16[672,512]{1,0:T(8,128)(2,1)S(1)} %collective-permute-done.52.refs_2_, ...), custom_call_target="tpu_custom_call" | custom-call | flops 4227858432 | bytes 13762560 | tf_op jit(solution)/shard_map/pallas_call | solution.py:249
  432.6 11.9 %shard_map.160 = bf16[768,512]{1,0:T(8,128)(2,1)} custom-call(s32[3]{0:T(128)} %pad_add_fusion.2.place_ref, bf16[768,512]{1,0:T(8,128)(2,1)} %copy-done.12, bf16[256,512]{1,0:T(8,128)(2,1)} %copy-done.53, bf16[768,512]{1,0:T(8,128)(2,1)} %copy-done.52, bf16[768,512]{1,0:T(8,128)(2,1)} %copy-done.24), custom_call_target="tpu_custom_call" | custom-call | flops 1811939328 | bytes 1572864 | tf_op jit(solution)/shard_map/pallas_call | solution.py:375
  444.5 4.1 collective-permute-start.60
  451.0 5.2 %collective-permute-done.60.refs_7_ = bf16[64,2688]{1,0:T(8,128)(2,1)S(1)} collective-permute-done((bf16[64,2688]{1,0:T(8,128)(2,1)S(1)}, bf16[64,2688]{1,0:T(8,128)(2,1)S(1)}, u32[]{:S(2)}, u32[]{:S(2)}) %collective-permute-start.60) | collective-permute-done | bytes 344096 | tf_op jit(solution)/shard_map/ppermute | solution.py:179
  456.7 4.9 collective-permute-done.61.refs_8_
  465.3 8.3 %collective-permute-done.85.refs_20_ = bf16[384,512]{1,0:T(8,128)(2,1)S(1)} collective-permute-done((bf16[384,512]{1,0:T(8,128)(2,1)S(1)}, bf16[384,512]{1,0:T(8,128)(2,1)S(1)}, u32[]{:S(2)}, u32[]{:S(2)}) %collective-permute-start.85) | collective-permute-done | bytes 393248 | tf_op jit(solution)/shard_map/ppermute | solution.py:560
  473.6 7.3 %collective-permute-done.86.refs_21_ = bf16[384,512]{1,0:T(8,128)(2,1)S(1)} collective-permute-done((bf16[384,512]{1,0:T(8,128)(2,1)S(1)}, bf16[384,512]{1,0:T(8,128)(2,1)S(1)}, u32[]{:S(2)}, u32[]{:S(2)}) %collective-permute-start.86) | collective-permute-done | bytes 393248 | tf_op jit(solution)/shard_map/ppermute | solution.py:561
  480.9 9.9 %shard_map.161 = (f32[384,2688]{1,0:T(8,128)S(1)}, f32[384,128]{1,0:T(8,128)S(1)}) custom-call(s32[22]{0:T(128)S(1)} %stack.80.at_ref, bf16[128,2688]{1,0:T(8,128)(2,1)S(1)} %copy-done.17, bf16[128,2688]{1,0:T(8,128)(2,1)} %collective-permute-done.54.refs_1_, bf16[128,2688]{1,0:T(8,128)(2,1)} %collective-permute-done.55.refs_2_, ...), custom_call_target="tpu_custom_call" | custom-call | flops 4227858432 | bytes 16515072 | tf_op jit(solution)/shard_map/pallas_call | solution.py:307
  (346 shorter events, 159.8 us)
Async XLA Ops:
  0.0 60.7 %collective-permute-start.31 = (bf16[384,2688]{1,0:T(8,128)(2,1)}, bf16[384,2688]{1,0:T(8,128)(2,1)}, u32[]{:S(2)}, u32[]{:S(2)}) collective-permute-start(bf16[384,2688]{1,0:T(8,128)(2,1)} %refs_9_.3), channel_id=1, source_target_pairs={{0,1},{1,0},{2,3},{3,2},{4,5},{5,4},{6,7},{7,6},{8,9},{9,8},{10,11... | collective-permute-start | bytes 6193160 | tf_op jit(solution)/shard_map/ppermute | solution.py:518
  1.5 101.6 %collective-permute-start.32 = (bf16[384,2688]{1,0:T(8,128)(2,1)}, bf16[384,2688]{1,0:T(8,128)(2,1)S(1)}, u32[]{:S(2)}, u32[]{:S(2)}) collective-permute-start(bf16[384,2688]{1,0:T(8,128)(2,1)} %refs_9_.3), channel_id=1, source_target_pairs={{0,2},{2,0},{4,6},{6,4},{8,10},{10,8},{12,14},{14,12},{16,18},{18,... | collective-permute-start | bytes 6193160 | tf_op jit(solution)/shard_map/ppermute | solution.py:519
  21.6 36.4 %collective-permute-start.34 = (bf16[336,512]{1,0:T(8,128)(2,1)}, bf16[336,512]{1,0:T(8,128)(2,1)}, u32[]{:S(2)}, u32[]{:S(2)}) collective-permute-start(bf16[336,512]{1,0:T(8,128)(2,1)} %pad_maximum_fusion.3), channel_id=1, source_target_pairs={{0,2},{2,0},{4,6},{6,4},{8,10},{10,8},{12,14},{14,12},{16,18},{18,... | collective-permute-start | bytes 1032200 | tf_op jit(solution)/shard_map/ppermute | solution.py:477
  60.7 78.4 %collective-permute-start.33 = (bf16[384,2688]{1,0:T(8,128)(2,1)}, bf16[384,2688]{1,0:T(8,128)(2,1)}, u32[]{:S(2)}, u32[]{:S(2)}) collective-permute-start(bf16[384,2688]{1,0:T(8,128)(2,1)} %collective-permute-done.31.refs_10_), channel_id=1, source_target_pairs={{0,2},{2,0},{4,6},{6,4},{8,10},{10,8},{12,14},{14,12},{16,18},{18,... | collective-permute-start | bytes 6193160 | tf_op jit(solution)/shard_map/ppermute | solution.py:520
  71.3 28.7 %collective-permute-start.7 = (bf16[672,512]{1,0:T(8,128)(2,1)}, bf16[672,512]{1,0:T(8,128)(2,1)}, u32[]{:S(2)}, u32[]{:S(2)}) collective-permute-start(bf16[672,512]{1,0:T(8,128)(2,1)} %collective-permute-done.6.refs_1_), channel_id=1, source_target_pairs={{0,4},{2,6},{4,12},{6,14},{12,20},{14,22},{20,28},{22,30},{28,24},... | collective-permute-start | bytes 2064392 | tf_op jit(solution)/shard_map/ppermute | solution.py:173
  73.5 27.0 %collective-permute-start.9 = (bf16[672,512]{1,0:T(8,128)(2,1)}, bf16[672,512]{1,0:T(8,128)(2,1)}, u32[]{:S(2)}, u32[]{:S(2)}) collective-permute-start(bf16[672,512]{1,0:T(8,128)(2,1)} %collective-permute-done.8.refs_2_), channel_id=1, source_target_pairs={{4,0},{6,2},{12,4},{14,6},{20,12},{22,14},{28,20},{30,22},{24,28},... | collective-permute-start | bytes 2064392 | tf_op jit(solution)/shard_map/ppermute | solution.py:174
  100.0 25.9 %collective-permute-start.27 = (bf16[672,512]{1,0:T(8,128)(2,1)}, bf16[672,512]{1,0:T(8,128)(2,1)S(1)}, u32[]{:S(2)}, u32[]{:S(2)}) collective-permute-start(bf16[672,512]{1,0:T(8,128)(2,1)} %collective-permute-done.7.refs_3_), channel_id=1, source_target_pairs={{0,4},{2,6},{4,12},{6,14},{12,20},{14,22},{20,28},{22,30},{28,24},... | collective-permute-start | bytes 2064392 | tf_op jit(solution)/shard_map/ppermute | solution.py:173
  100.6 26.0 %collective-permute-start.28 = (bf16[672,512]{1,0:T(8,128)(2,1)}, bf16[672,512]{1,0:T(8,128)(2,1)S(1)}, u32[]{:S(2)}, u32[]{:S(2)}) collective-permute-start(bf16[672,512]{1,0:T(8,128)(2,1)} %collective-permute-done.9.refs_4_), channel_id=1, source_target_pairs={{4,0},{6,2},{12,4},{14,6},{20,12},{22,14},{28,20},{30,22},{24,28},... | collective-permute-start | bytes 2064392 | tf_op jit(solution)/shard_map/ppermute | solution.py:174
  106.8 32.3 %collective-permute-start.10 = (bf16[128,2688]{1,0:T(8,128)(2,1)}, bf16[128,2688]{1,0:T(8,128)(2,1)}, u32[]{:S(2)}, u32[]{:S(2)}) collective-permute-start(bf16[128,2688]{1,0:T(8,128)(2,1)} %get-tuple-element.25.refs_0_), channel_id=1, source_target_pairs={{0,4},{2,6},{4,12},{6,14},{12,20},{14,22},{20,28},{22,30},{28,24},... | collective-permute-start | bytes 2064392 | tf_op jit(solution)/shard_map/ppermute | solution.py:173
  125.9 28.0 %collective-permute-start.18 = (bf16[128,2688]{1,0:T(8,128)(2,1)}, bf16[128,2688]{1,0:T(8,128)(2,1)S(1)}, u32[]{:S(2)}, u32[]{:S(2)}) collective-permute-start(bf16[128,2688]{1,0:T(8,128)(2,1)} %get-tuple-element.25.refs_0_), channel_id=1, source_target_pairs={{0,2},{2,0},{4,6},{6,4},{8,10},{10,8},{12,14},{14,12},{16,18},{18,... | collective-permute-start | bytes 2064392 | tf_op jit(solution)/shard_map/ppermute | solution.py:566
  126.6 31.4 %collective-permute-start.11 = (bf16[128,2688]{1,0:T(8,128)(2,1)}, bf16[128,2688]{1,0:T(8,128)(2,1)}, u32[]{:S(2)}, u32[]{:S(2)}) collective-permute-start(bf16[128,2688]{1,0:T(8,128)(2,1)} %get-tuple-element.25.refs_0_), channel_id=1, source_target_pairs={{4,0},{6,2},{12,4},{14,6},{20,12},{22,14},{28,20},{30,22},{24,28},... | collective-permute-start | bytes 2064392 | tf_op jit(solution)/shard_map/ppermute | solution.py:174
  154.7 32.5 %collective-permute-start.41 = (bf16[768,512]{1,0:T(8,128)(2,1)}, bf16[768,512]{1,0:T(8,128)(2,1)}, u32[]{:S(2)}, u32[]{:S(2)}) collective-permute-start(bf16[768,512]{1,0:T(8,128)(2,1)} %get-tuple-element.29.refs_2_), channel_id=1, source_target_pairs={{0,4},{2,6},{4,8},{6,10},{8,12},{10,14},{12,16},{14,18},{16,20},{1... | collective-permute-start | bytes 2359304 | tf_op jit(solution)/shard_map/ppermute | solution.py:541
  158.0 27.7 %collective-permute-start.19 = (bf16[128,2688]{1,0:T(8,128)(2,1)}, bf16[128,2688]{1,0:T(8,128)(2,1)S(1)}, u32[]{:S(2)}, u32[]{:S(2)}) collective-permute-start(bf16[128,2688]{1,0:T(8,128)(2,1)} %collective-permute-done.10.refs_1_), channel_id=1, source_target_pairs={{0,2},{2,0},{4,6},{6,4},{8,10},{10,8},{12,14},{14,12},{16,18},{18,... | collective-permute-start | bytes 2064392 | tf_op jit(solution)/shard_map/ppermute | solution.py:566
  158.0 27.2 %collective-permute-start.13 = (bf16[128,2688]{1,0:T(8,128)(2,1)}, bf16[128,2688]{1,0:T(8,128)(2,1)}, u32[]{:S(2)}, u32[]{:S(2)}) collective-permute-start(bf16[128,2688]{1,0:T(8,128)(2,1)} %collective-permute-done.11.refs_2_), channel_id=1, source_target_pairs={{4,0},{6,2},{12,4},{14,6},{20,12},{22,14},{28,20},{30,22},{24,28},... | collective-permute-start | bytes 2064392 | tf_op jit(solution)/shard_map/ppermute | solution.py:174
  164.2 36.0 %collective-permute-start.14 = (bf16[128,2688]{1,0:T(8,128)(2,1)}, bf16[128,2688]{1,0:T(8,128)(2,1)}, u32[]{:S(2)}, u32[]{:S(2)}) collective-permute-start(bf16[128,2688]{1,0:T(8,128)(2,1)} %collective-permute-done.12.refs_3_), channel_id=1, source_target_pairs={{0,4},{2,6},{4,12},{6,14},{12,20},{14,22},{20,28},{22,30},{28,24},... | collective-permute-start | bytes 2064392 | tf_op jit(solution)/shard_map/ppermute | solution.py:173
  185.2 26.1 %collective-permute-start.21 = (bf16[128,2688]{1,0:T(8,128)(2,1)}, bf16[128,2688]{1,0:T(8,128)(2,1)}, u32[]{:S(2)}, u32[]{:S(2)}) collective-permute-start(bf16[128,2688]{1,0:T(8,128)(2,1)} %collective-permute-done.12.refs_3_), channel_id=1, source_target_pairs={{0,2},{2,0},{4,6},{6,4},{8,10},{10,8},{12,14},{14,12},{16,18},{18,... | collective-permute-start | bytes 2064392 | tf_op jit(solution)/shard_map/ppermute | solution.py:566
  247.0 44.7 %collective-permute-start.75 = (bf16[384,2688]{1,0:T(8,128)(2,1)S(1)}, bf16[384,2688]{1,0:T(8,128)(2,1)S(1)}, u32[]{:S(2)}, u32[]{:S(2)}) collective-permute-start(bf16[384,2688]{1,0:T(8,128)(2,1)S(1)} %add_convert_fusion.1.refs_9_), channel_id=1, source_target_pairs={{0,1},{1,0},{2,3},{3,2},{4,5},{5,4},{6,7},{7,6},{8,9},{9,8},{10,11... | collective-permute-start | bytes 6193160 | tf_op jit(solution)/shard_map/ppermute | solution.py:518
  277.9 81.6 %collective-permute-start.76 = (bf16[384,2688]{1,0:T(8,128)(2,1)S(1)}, bf16[384,2688]{1,0:T(8,128)(2,1)S(1)}, u32[]{:S(2)}, u32[]{:S(2)}) collective-permute-start(bf16[384,2688]{1,0:T(8,128)(2,1)S(1)} %add_convert_fusion.1.refs_9_), channel_id=1, source_target_pairs={{0,2},{2,0},{4,6},{6,4},{8,10},{10,8},{12,14},{14,12},{16,18},{18,... | collective-permute-start | bytes 6193160 | tf_op jit(solution)/shard_map/ppermute | solution.py:519
  291.7 69.5 %collective-permute-start.77 = (bf16[384,2688]{1,0:T(8,128)(2,1)S(1)}, bf16[384,2688]{1,0:T(8,128)(2,1)S(1)}, u32[]{:S(2)}, u32[]{:S(2)}) collective-permute-start(bf16[384,2688]{1,0:T(8,128)(2,1)S(1)} %collective-permute-done.75.refs_10_), channel_id=1, source_target_pairs={{0,2},{2,0},{4,6},{6,4},{8,10},{10,8},{12,14},{14,12},{16,18},{18,... | collective-permute-start | bytes 6193160 | tf_op jit(solution)/shard_map/ppermute | solution.py:520
  305.9 32.2 %collective-permute-start.78 = (bf16[672,512]{1,0:T(8,128)(2,1)S(1)}, bf16[672,512]{1,0:T(8,128)(2,1)S(1)}, u32[]{:S(2)}, u32[]{:S(2)}) collective-permute-start(bf16[672,512]{1,0:T(8,128)(2,1)S(1)} %collective-permute-done.47.refs_3_), channel_id=1, source_target_pairs={{0,4},{2,6},{4,12},{6,14},{12,20},{14,22},{20,28},{22,30},{28,24},... | collective-permute-start | bytes 2064392 | tf_op jit(solution)/shard_map/ppermute | solution.py:173
  306.4 32.7 %collective-permute-start.79 = (bf16[672,512]{1,0:T(8,128)(2,1)S(1)}, bf16[672,512]{1,0:T(8,128)(2,1)S(1)}, u32[]{:S(2)}, u32[]{:S(2)}) collective-permute-start(bf16[672,512]{1,0:T(8,128)(2,1)S(1)} %collective-permute-done.49.refs_4_), channel_id=1, source_target_pairs={{4,0},{6,2},{12,4},{14,6},{20,12},{22,14},{28,20},{30,22},{24,28},... | collective-permute-start | bytes 2064392 | tf_op jit(solution)/shard_map/ppermute | solution.py:174
  323.5 37.7 %collective-permute-start.56 = (bf16[128,2688]{1,0:T(8,128)(2,1)}, bf16[128,2688]{1,0:T(8,128)(2,1)}, u32[]{:S(2)}, u32[]{:S(2)}) collective-permute-start(bf16[128,2688]{1,0:T(8,128)(2,1)} %collective-permute-done.54.refs_1_), channel_id=1, source_target_pairs={{0,4},{2,6},{4,12},{6,14},{12,20},{14,22},{20,28},{22,30},{28,24},... | collective-permute-start | bytes 2064392 | tf_op jit(solution)/shard_map/ppermute | solution.py:173
  359.4 28.3 %collective-permute-start.72 = (bf16[672,512]{1,0:T(8,128)(2,1)S(1)}, bf16[672,512]{1,0:T(8,128)(2,1)S(1)}, u32[]{:S(2)}, u32[]{:S(2)}) collective-permute-start(bf16[672,512]{1,0:T(8,128)(2,1)S(1)} %collective-permute-done.53.refs_4_), channel_id=1, source_target_pairs={{4,0},{6,2},{12,4},{14,6},{20,12},{22,14},{28,20},{30,22},{24,28},... | collective-permute-start | bytes 2064392 | tf_op jit(solution)/shard_map/ppermute | solution.py:174
  361.2 30.4 %collective-permute-start.62 = (bf16[128,2688]{1,0:T(8,128)(2,1)S(1)}, bf16[128,2688]{1,0:T(8,128)(2,1)S(1)}, u32[]{:S(2)}, u32[]{:S(2)}) collective-permute-start(bf16[128,2688]{1,0:T(8,128)(2,1)S(1)} %copy-done.16), channel_id=1, source_target_pairs={{0,2},{2,0},{4,6},{6,4},{8,10},{10,8},{12,14},{14,12},{16,18},{18,... | collective-permute-start | bytes 2064392 | tf_op jit(solution)/shard_map/ppermute | solution.py:566
  361.2 51.6 %collective-permute-start.58 = (bf16[128,2688]{1,0:T(8,128)(2,1)}, bf16[128,2688]{1,0:T(8,128)(2,1)S(1)}, u32[]{:S(2)}, u32[]{:S(2)}) collective-permute-start(bf16[128,2688]{1,0:T(8,128)(2,1)} %collective-permute-done.56.refs_3_), channel_id=1, source_target_pairs={{0,4},{2,6},{4,12},{6,14},{12,20},{14,22},{20,28},{22,30},{28,24},... | collective-permute-start | bytes 2064392 | tf_op jit(solution)/shard_map/ppermute | solution.py:173
  375.5 44.4 %collective-permute-start.83 = (bf16[768,512]{1,0:T(8,128)(2,1)S(1)}, bf16[768,512]{1,0:T(8,128)(2,1)S(1)}, u32[]{:S(2)}, u32[]{:S(2)}) collective-permute-start(bf16[768,512]{1,0:T(8,128)(2,1)S(1)} %get-tuple-element.36.refs_2_), channel_id=1, source_target_pairs={{0,4},{2,6},{4,8},{6,10},{8,12},{10,14},{12,16},{14,18},{16,20},{1... | collective-permute-start | bytes 2359304 | tf_op jit(solution)/shard_map/ppermute | solution.py:541
  378.4 37.0 %collective-permute-start.57 = (bf16[128,2688]{1,0:T(8,128)(2,1)}, bf16[128,2688]{1,0:T(8,128)(2,1)}, u32[]{:S(2)}, u32[]{:S(2)}) collective-permute-start(bf16[128,2688]{1,0:T(8,128)(2,1)} %collective-permute-done.55.refs_2_), channel_id=1, source_target_pairs={{4,0},{6,2},{12,4},{14,6},{20,12},{22,14},{28,20},{30,22},{24,28},... | collective-permute-start | bytes 2064392 | tf_op jit(solution)/shard_map/ppermute | solution.py:174
  412.8 31.7 %collective-permute-start.63 = (bf16[128,2688]{1,0:T(8,128)(2,1)}, bf16[128,2688]{1,0:T(8,128)(2,1)}, u32[]{:S(2)}, u32[]{:S(2)}) collective-permute-start(bf16[128,2688]{1,0:T(8,128)(2,1)} %collective-permute-done.54.refs_1_), channel_id=1, source_target_pairs={{0,2},{2,0},{4,6},{6,4},{8,10},{10,8},{12,14},{14,12},{16,18},{18,... | collective-permute-start | bytes 2064392 | tf_op jit(solution)/shard_map/ppermute | solution.py:566
  414.9 36.0 %collective-permute-start.64 = (bf16[128,2688]{1,0:T(8,128)(2,1)}, bf16[128,2688]{1,0:T(8,128)(2,1)}, u32[]{:S(2)}, u32[]{:S(2)}) collective-permute-start(bf16[128,2688]{1,0:T(8,128)(2,1)} %collective-permute-done.55.refs_2_), channel_id=1, source_target_pairs={{0,2},{2,0},{4,6},{6,4},{8,10},{10,8},{12,14},{14,12},{16,18},{18,... | collective-permute-start | bytes 2064392 | tf_op jit(solution)/shard_map/ppermute | solution.py:566
  415.4 40.7 %collective-permute-start.65 = (bf16[128,2688]{1,0:T(8,128)(2,1)}, bf16[128,2688]{1,0:T(8,128)(2,1)}, u32[]{:S(2)}, u32[]{:S(2)}) collective-permute-start(bf16[128,2688]{1,0:T(8,128)(2,1)} %collective-permute-done.56.refs_3_), channel_id=1, source_target_pairs={{0,2},{2,0},{4,6},{6,4},{8,10},{10,8},{12,14},{14,12},{16,18},{18,... | collective-permute-start | bytes 2064392 | tf_op jit(solution)/shard_map/ppermute | solution.py:566
  418.2 31.6 %collective-permute-start.59 = (bf16[128,2688]{1,0:T(8,128)(2,1)}, bf16[128,2688]{1,0:T(8,128)(2,1)}, u32[]{:S(2)}, u32[]{:S(2)}) collective-permute-start(bf16[128,2688]{1,0:T(8,128)(2,1)} %collective-permute-done.57.refs_4_), channel_id=1, source_target_pairs={{4,0},{6,2},{12,4},{14,6},{20,12},{22,14},{28,20},{30,22},{24,28},... | collective-permute-start | bytes 2064392 | tf_op jit(solution)/shard_map/ppermute | solution.py:174
  420.0 36.6 %collective-permute-start.66 = (bf16[128,2688]{1,0:T(8,128)(2,1)}, bf16[128,2688]{1,0:T(8,128)(2,1)}, u32[]{:S(2)}, u32[]{:S(2)}) collective-permute-start(bf16[128,2688]{1,0:T(8,128)(2,1)} %collective-permute-done.57.refs_4_), channel_id=1, source_target_pairs={{0,2},{2,0},{4,6},{6,4},{8,10},{10,8},{12,14},{14,12},{16,18},{18,... | collective-permute-start | bytes 2064392 | tf_op jit(solution)/shard_map/ppermute | solution.py:566
  (113 other events, 1534.1 us)
